TPU v7x, 32 devices: a whole 2x2x4 slice. The times are simulated.
32 devices in a mesh: groups: 2 (over y), grid: 16 (over z, x, core).
Axes of the slice: x: 2, y: 2, z: 4, core: 2. Of those that a mesh axis runs over, the one named last changes fastest.
Arguments:
- start_field: float32 [32, 1024, 128], P(('groups', 'grid')), parts along dimension 0, may hold values from -6 to 6
- col_speed: float32 [1024], replicated, may hold values from 0.5 to 2
- row_speed: float32 [32], replicated, may hold values from 0.5 to 2
- levels: int32 [32], P('groups'), parts along dimension 0, may hold values from 2 to 5, as said below
- coeffs: int32 [32], P('groups'), parts along dimension 0, may hold values from 1 to 3
- assign_first: int32 [32], P('groups'), parts along dimension 0, may hold values from 0 to 15, each once
- assign_second: int32 [32], P('groups'), parts along dimension 0, may hold values from 0 to 15, each once
- owner_of: int32 [32], P('groups'), parts along dimension 0, may hold values from 0 to 15, each once
Outputs:
- combined: float32 [2048, 1280], P(('groups', 'grid')), parts along dimension 0
- final_field: float32 [32, 1024, 128], P(('groups', 'grid')), parts along dimension 0
There are 2 independent parts, one for each index of `groups`. A program takes and returns all parts, laid end to end along the dimension named above; an argument that names none is the same for every part. Nothing has to cross between parts.
Inputs may be any that keep to these rules, and one draw needn't show every extreme that they name: `levels`: every run of 4 consecutive grids starting at a multiple of 4 holds each first level from 2 to 5 exactly once.
All inputs are finite; a program needn't handle non-finite values.
Results may differ from a plain program's by a relative error of at most 0.0003.
Values sent between devices are 32-bit elements; how exact they have to be, the bound alone decides.
A program may use at most 64 MiB of HBM per device.

v0:
```python
import jax
import jax.numpy as jnp
import numpy as np
from jax import lax
from jax.sharding import PartitionSpec as P

LMIN = 2
NLEV = 4
CLEV = 5
STEPS = 2


time_step = 0.02
diffusivity = 0.0024
highest = lax.Precision.HIGHEST


def hier_line(line_level):
    points = 2**line_level
    matrix = np.zeros((points, points))
    matrix[0, 0] = 1.0
    for tier_rank in range(1, line_level + 1):
        stride = 2 ** (line_level - tier_rank)
        for entry_at in range(2 ** (tier_rank - 1), 2**tier_rank):
            node_at = (2 * (entry_at - 2 ** (tier_rank - 1)) + 1) * stride
            matrix[entry_at, node_at] += 1.0
            matrix[entry_at, (node_at - stride) % points] -= 0.5
            matrix[entry_at, (node_at + stride) % points] -= 0.5
    return matrix


def dehier_line(line_level):
    points = 2**line_level
    matrix = np.zeros((points, points))
    matrix[0, 0] = 1.0
    for tier_rank in range(1, line_level + 1):
        stride = 2 ** (line_level - tier_rank)
        for entry_at in range(2 ** (tier_rank - 1), 2**tier_rank):
            node_at = (2 * (entry_at - 2 ** (tier_rank - 1)) + 1) * stride
            matrix[node_at] = 0.5 * (
                matrix[(node_at - stride) % points] + matrix[(node_at + stride) % points]
            )
            matrix[node_at, entry_at] += 1.0
    return matrix


def row_tables():
    row_bits = 2 * LMIN + NLEV - 1
    starts, widths, offsets = ([], [], [])
    running = 0
    for piece_level in range(LMIN, LMIN + NLEV):
        first_row = 0 if piece_level == LMIN else 2 ** (piece_level - 1)
        breadth = 2**LMIN if piece_level == LMIN else 2 ** (piece_level - 1)
        starts.append(first_row)
        widths.append(breadth)
        offsets.append(running)
        running += breadth * 2 ** (row_bits - piece_level)
    forward, backward, embeds, places = ([], [], [], [])
    for shift_level in range(NLEV):
        first_level = LMIN + shift_level
        second_level = row_bits - first_level
        tensor = np.kron(hier_line(first_level), hier_line(second_level))
        inverse = np.kron(dehier_line(first_level), dehier_line(second_level))
        order_list, place_list = ([], [])
        for slot_index in range(shift_level + 1):
            for second in range(2**second_level):
                for first_idx in range(starts[slot_index], starts[slot_index] + widths[slot_index]):
                    order_list.append(first_idx * 2**second_level + second)
                    place_list.append(
                        offsets[slot_index]
                        + second * widths[slot_index]
                        + first_idx
                        - starts[slot_index]
                    )
        embedding = np.zeros((running, 2**row_bits))
        embedding[np.array(place_list), np.arange(2**row_bits)] = 1.0
        forward.append(tensor[order_list])
        backward.append(inverse[:, order_list])
        embeds.append(embedding)
        places.append(place_list)
    return (
        jnp.asarray(np.stack(forward), jnp.float32),
        jnp.asarray(np.stack(backward), jnp.float32),
        jnp.asarray(np.stack(embeds), jnp.float32),
        jnp.asarray(np.array(places), jnp.int32),
    )


def column_pass(values, matrix):
    side_cells = matrix.shape[0]
    cube_view = values.reshape(side_cells, side_cells, values.shape[-1])
    cube_view = jnp.einsum("ab,bjr->ajr", matrix, cube_view, precision=highest)
    cube_view = jnp.einsum("ab,jbr->jar", matrix, cube_view, precision=highest)
    return cube_view.reshape(values.shape)


def advance(values, grid_level, count, col_speed, row_speed):
    side_cells = 2**CLEV
    total_rows = values.shape[1]
    row_bits = 2 * LMIN + NLEV - 1
    other_level = row_bits - grid_level
    inner_count = jnp.left_shift(jnp.int32(1), other_level)
    inner_pos = jnp.bitwise_and(jnp.arange(total_rows, dtype=jnp.int32), inner_count - 1)
    sample_at = inner_pos * jnp.left_shift(jnp.int32(1), row_bits - LMIN - other_level)
    fine_cells = row_speed.shape[0]
    row_factor = jnp.sum(
        jnp.where(
            sample_at[:, None] == jnp.arange(fine_cells, dtype=jnp.int32)[None, :],
            row_speed[None, :],
            jnp.zeros_like(row_speed)[None, :],
        ),
        axis=1,
    )
    velocity = col_speed[:, None] * row_factor[None, :]
    refine = jnp.left_shift(jnp.int32(1), grid_level - LMIN)
    dt_sub = time_step / refine.astype(jnp.float32)
    scale_one = jnp.left_shift(jnp.int32(1), grid_level).astype(jnp.float32)
    scale_two = inner_count.astype(jnp.float32)
    coeff_side = float(4**CLEV)
    at_last = (inner_pos == inner_count - 1)[None, :]
    at_first = (inner_pos == 0)[None, :]

    def one_substep(turn_index, current):
        up_one = jnp.roll(current, -inner_count, axis=1)
        down_one = jnp.roll(current, inner_count, axis=1)
        up_two = jnp.where(
            at_last, jnp.roll(current, inner_count - 1, axis=1), jnp.roll(current, -1, axis=1)
        )
        down_two = jnp.where(
            at_first, jnp.roll(current, 1 - inner_count, axis=1), jnp.roll(current, 1, axis=1)
        )
        cube_view = current.reshape(side_cells, side_cells, total_rows)
        across = (
            jnp.roll(cube_view, 1, axis=0)
            + jnp.roll(cube_view, -1, axis=0)
            + jnp.roll(cube_view, 1, axis=1)
            + jnp.roll(cube_view, -1, axis=1)
        )
        across = across.reshape(current.shape) - 4.0 * current
        spread = (
            scale_one * scale_one * (up_one + down_one - 2.0 * current)
            + scale_two * scale_two * (up_two + down_two - 2.0 * current)
            + coeff_side * across
        )
        transport = velocity * (up_one - down_one) * (0.5 * scale_one)
        return current + dt_sub * (diffusivity * spread - transport)

    return lax.fori_loop(jnp.int32(0), refine * count, one_substep, values)


def local(start_field, col_speed, row_speed, levels, coeffs, assign_first, assign_second, owner_of):
    forward, backward, embeds, places = row_tables()
    column_hier = jnp.asarray(hier_line(CLEV), jnp.float32)
    column_back = jnp.asarray(dehier_line(CLEV), jnp.float32)
    cover = jnp.sum(embeds, axis=2)
    section_rows = embeds.shape[1]
    devices = lax.axis_size("grid")
    my_index = lax.axis_index("grid")
    grid_count = levels.shape[0]
    total_cols = start_field.shape[1]
    total_rows = start_field.shape[2]
    block_cols = total_cols // devices
    sections = devices // NLEV
    grid_ids = jnp.arange(grid_count, dtype=jnp.int32)
    section_ids = jnp.arange(sections, dtype=jnp.int32)
    level_ids = LMIN + jnp.arange(NLEV, dtype=jnp.int32)
    weights = coeffs.astype(jnp.float32)
    section_all = (grid_ids[:, None] // NLEV == section_ids[None, :]).astype(jnp.float32)
    level_all = (levels[:, None] == level_ids[None, :]).astype(jnp.float32) * weights[:, None]
    denominator = jnp.dot(
        jnp.dot(section_all.T, level_all, precision=highest), cover, precision=highest
    )

    def holders(assignment):
        return jnp.sum(
            jnp.where(assignment[None, :] == grid_ids[:, None], grid_ids[None, :], 0), axis=1
        )

    def lookup(table, wanted):
        return jnp.sum(
            jnp.where(
                wanted[:, None] == grid_ids[None, :], table[None, :], jnp.zeros_like(table)[None, :]
            ),
            axis=1,
        )

    def pick_entry(table, wanted):
        return jnp.sum(jnp.where(grid_ids == wanted, table, jnp.zeros_like(table)))

    owner_inv = holders(owner_of)
    first_grids = holders(assign_first)
    second_grids = holders(assign_second)
    own_first = pick_entry(first_grids, my_index)
    own_second = pick_entry(second_grids, my_index)
    level_first = pick_entry(levels, own_first)
    level_second = pick_entry(levels, own_second)
    weight_first = pick_entry(weights, own_first)
    weight_second = pick_entry(weights, own_second)

    def hierarchize(values, grid_level):
        mixed = column_pass(values, column_hier)
        return jnp.dot(mixed, forward[grid_level - LMIN].T, precision=highest)

    def dehierarchize(values, grid_level):
        mixed = jnp.dot(values, backward[grid_level - LMIN].T, precision=highest)
        return column_pass(mixed, column_back)

    def combine(surplus, my_weight, sender_grids):
        blocks = (surplus * my_weight).reshape(devices, block_cols, total_rows)
        outgoing = jnp.take(blocks, owner_inv, axis=0)
        source_levels = lookup(levels, sender_grids)
        section_hot = (sender_grids[:, None] // NLEV == section_ids[None, :]).astype(jnp.float32)
        incoming = lax.all_to_all(outgoing, "grid", split_axis=0, concat_axis=0, tiled=True)
        total = jnp.zeros((block_cols, sections, section_rows), jnp.float32)
        for shift_level in range(NLEV):
            level_mask = (
                section_hot * (source_levels == LMIN + shift_level).astype(jnp.float32)[:, None]
            )
            grouped = jnp.einsum("skr,sp->kpr", incoming, level_mask, precision=highest)
            total = total + jnp.einsum(
                "kpr,cr->kpc", grouped, embeds[shift_level], precision=highest
            )
        return total / denominator[None, :, :]

    def give_back(section_values, dest_grids, my_level):
        dest_sections = dest_grids // NLEV
        picked = jnp.take(section_values, dest_sections, axis=1)
        incoming = lax.all_to_all(picked, "grid", split_axis=1, concat_axis=0, tiled=True)
        arranged = incoming.reshape(devices, block_cols, section_rows)
        ordered = jnp.take(arranged, owner_of, axis=0).reshape(total_cols, section_rows)
        return jnp.take(ordered, places[my_level - LMIN], axis=1)

    current = advance(start_field[0], level_first, STEPS, col_speed, row_speed)
    first_combined = combine(hierarchize(current, level_first), weight_first, first_grids)
    restricted = give_back(first_combined, second_grids, level_second)
    current = advance(
        dehierarchize(restricted, level_second), level_second, STEPS, col_speed, row_speed
    )
    second_combined = combine(hierarchize(current, level_second), weight_second, second_grids)
    restricted = give_back(second_combined, second_grids, level_second)
    current = advance(
        dehierarchize(restricted, level_second), level_second, 1, col_speed, row_speed
    )
    return (second_combined.reshape(block_cols, sections * section_rows), current[None])


def solution(mesh):
    placed = (
        P(("groups", "grid"), None, None),
        P(),
        P(),
        P("groups"),
        P("groups"),
        P("groups"),
        P("groups"),
        P("groups"),
    )
    return jax.shard_map(
        local,
        mesh=mesh,
        in_specs=placed,
        out_specs=(P(("groups", "grid"), None), P(("groups", "grid"), None, None)),
        check_vma=False,
    )
```

profile of v0, /device:TPU:24, one launch (start us, length us, event | category | flops | bytes accessed | tf_op | source)
XLA Modules:
  0.0 264.8 jit_solution(7163760308921973153)
XLA Ops:
  0.6 1.0 copy.170
  4.7 2.7 %fusion.160 = (s32[]{:T(128)}, s32[]{:T(128)}) fusion(s32[16]{0:T(128)} %param.33, s32[]{:T(128)} %get-tuple-element.796, s32[]{:T(128)} %get-tuple-element.793), kind=kLoop, calls=%fused_computation.274 | loop fusion | flops 94 | bytes 80 | tf_op jit(solution)/shard_map/reduce_sum | solution.py:188
  10.4 2.6 fusion.161
  13.8 5.3 %while.42 = (s32[]{:T(128)}, f32[1024,128]{1,0:T(8,128)S(1)}, s32[]{:T(128)}, f32[]{:T(128)}, f32[]{:T(128)}, /*index=5*/s32[]{:T(128)}, s32[]{:T(128)}, f32[]{:...) while((s32[]{:T(128)}, f32[1024,128]{1,0:T(8,128)S(1)}, ...), condition=%wide.region_8.10_spmd.clone.clone, body=%wide.region_7.9_spmd.clone.clone.sunk | while | flops 4063678 | bytes 15750993 | solution.py:148
  20.9 2.0 convolution_multiply_fusion.1
  24.4 43.1 %all-to-all-start = ((f32[16,64,128]{2,1,0:T(8,128)}), f32[16,64,128]{2,1,0:T(8,128)S(1)}, u32[]{:S(2)}, u32[]{:S(2)}) async-start(f32[16,64,128]{2,1,0:T(8,128)} %broadcast_select_fusion.3), calls=%async_computation | async-start | bytes 1048576 | tf_op jit(solution)/shard_map/all_to_all | solution.py:213
  68.7 10.8 %all-to-all-done = f32[16,64,128]{2,1,0:T(8,128)S(1)} async-done(((f32[16,64,128]{2,1,0:T(8,128)}), f32[16,64,128]{2,1,0:T(8,128)S(1)}, u32[]{:S(2)}, u32[]{:S(2)}) %all-to-all-start) | async-done | bytes 524320 | tf_op jit(solution)/shard_map/all_to_all | solution.py:213
  84.7 1.4 select_bitcast_fusion.1
  86.1 6.6 %all-to-all-start.1 = ((f32[64,16,320]{2,0,1:T(8,128)}), f32[64,16,320]{2,0,1:T(8,128)S(1)}, u32[]{:S(2)}, u32[]{:S(2)}) async-start(f32[64,16,320]{2,0,1:T(8,128)} %select_bitcast_fusion.1), calls=%async_computation.1 | async-start | bytes 3145728 | tf_op jit(solution)/shard_map/all_to_all | solution.py:228
  95.6 29.9 %all-to-all-done.1 = f32[64,16,320]{2,0,1:T(8,128)S(1)} async-done(((f32[64,16,320]{2,0,1:T(8,128)}), f32[64,16,320]{2,0,1:T(8,128)S(1)}, u32[]{:S(2)}, u32[]{:S(2)}) %all-to-all-start.1) | async-done | bytes 1310752 | tf_op jit(solution)/shard_map/all_to_all | solution.py:228
  126.2 1.4 broadcast_select_fusion.1
  127.6 1.9 copy.77
  130.6 1.7 fusion.61
  133.8 34.5 %while.43 = (s32[]{:T(128)}, f32[1024,128]{1,0:T(8,128)S(1)}, s32[]{:T(128)}, f32[]{:T(128)}, f32[]{:T(128)}, /*index=5*/s32[]{:T(128)}, s32[]{:T(128)}, f32[]{:...) while((s32[]{:T(128)}, f32[1024,128]{1,0:T(8,128)S(1)}, ...), condition=%wide.region_16.22_spmd.clone.clone, body=%wide.region_15.21_spmd.clone.clone.sunk | while | flops 4063678 | bytes 15734581 | solution.py:148
  134.9 1.0 fusion.245
  137.1 1.0 fusion.245
  141.4 1.0 fusion.245
  145.7 1.0 fusion.245
  147.9 1.0 fusion.245
  150.0 1.0 fusion.245
  152.2 1.0 fusion.245
  154.3 1.0 fusion.245
  170.1 2.0 convolution_multiply_fusion
  173.6 7.0 %all-to-all-start.2 = ((f32[16,64,128]{2,1,0:T(8,128)}), f32[16,64,128]{2,1,0:T(8,128)S(1)}, u32[]{:S(2)}, u32[]{:S(2)}) async-start(f32[16,64,128]{2,1,0:T(8,128)} %broadcast_select_fusion.2), calls=%async_computation.2 | async-start | bytes 1048576 | tf_op jit(solution)/shard_map/all_to_all | solution.py:213
  180.6 12.0 %all-to-all-done.2 = f32[16,64,128]{2,1,0:T(8,128)S(1)} async-done(((f32[16,64,128]{2,1,0:T(8,128)}), f32[16,64,128]{2,1,0:T(8,128)S(1)}, u32[]{:S(2)}, u32[]{:S(2)}) %all-to-all-start.2) | async-done | bytes 524320 | tf_op jit(solution)/shard_map/all_to_all | solution.py:213
  197.8 1.4 select_bitcast_fusion
  199.2 6.4 %all-to-all-start.3 = ((f32[64,16,320]{2,0,1:T(8,128)}), f32[64,16,320]{2,0,1:T(8,128)S(1)}, u32[]{:S(2)}, u32[]{:S(2)}) async-start(f32[64,16,320]{2,0,1:T(8,128)} %select_bitcast_fusion), calls=%async_computation.3 | async-start | bytes 3145728 | tf_op jit(solution)/shard_map/all_to_all | solution.py:228
  206.9 31.6 %all-to-all-done.3 = f32[64,16,320]{2,0,1:T(8,128)S(1)} async-done(((f32[64,16,320]{2,0,1:T(8,128)}), f32[64,16,320]{2,0,1:T(8,128)S(1)}, u32[]{:S(2)}, u32[]{:S(2)}) %all-to-all-start.3) | async-done | bytes 1310752 | tf_op jit(solution)/shard_map/all_to_all | solution.py:228
  239.1 1.4 broadcast_select_fusion
  240.5 1.9 copy.92
  243.5 1.7 fusion.59
  246.8 17.2 %while.44 = (s32[]{:T(128)}, f32[1024,128]{1,0:T(8,128)S(1)}, s32[]{:T(128)}, f32[]{:T(128)}, f32[]{:T(128)}, /*index=5*/s32[]{:T(128)}, s32[]{:T(128)}, f32[]{:...) while((s32[]{:T(128)}, f32[1024,128]{1,0:T(8,128)S(1)}, ...), condition=%wide.region_19.25_spmd.clone.clone, body=%wide.region_18.24_spmd.clone.clone.sunk | while | flops 4063678 | bytes 15734581 | solution.py:148
  (391 shorter events, 74.9 us)
Async XLA Ops:
  13.8 5.3 %copy-start.9 = (f32[32,32,1]{1,0,2:T(8,128)S(1)}, f32[32,32,1]{1,0,2:T(8,128)}, u32[]{:S(2)}) copy-start(f32[32,32,1]{1,0,2:T(8,128)} %constant.249) | copy-start | bytes 12292
  14.7 0.7 copy-start.1
  17.3 0.7 copy-start.1
  22.9 44.6 %copy-start.19 = (s32[16]{0:T(128)S(1)}, s32[16]{0:T(128)}, u32[]{:S(2)}) copy-start(s32[16]{0:T(128)} %param.34) | copy-start | bytes 196
  22.9 44.7 %copy-start.13 = (s32[16]{0:T(128)S(1)}, s32[16]{0:T(128)}, u32[]{:S(2)}) copy-start(s32[16]{0:T(128)} %param.33) | copy-start | bytes 196
  22.9 45.6 %copy-start.10 = (f32[4,320]{1,0:T(4,128)S(1)}, f32[4,320]{1,0:T(4,128)}, u32[]{:S(2)}) copy-start(f32[4,320]{1,0:T(4,128)} %constant.248) | copy-start | bytes 15364
  23.5 56.7 %copy-start.3 = (f32[320,128,1]{1,0,2:T(8,128)S(1)}, f32[320,128,1]{1,0,2:T(8,128)}, u32[]{:S(2)}) copy-start(f32[320,128,1]{1,0,2:T(8,128)} %constant.251) | copy-start | bytes 491524
  24.4 56.9 %copy-start.5 = (f32[320,128,1]{1,0,2:T(8,128)S(1)}, f32[320,128,1]{1,0,2:T(8,128)}, u32[]{:S(2)}) copy-start(f32[320,128,1]{1,0,2:T(8,128)} %constant.252) | copy-start | bytes 491524
  24.4 55.1 %all-to-all-start = ((f32[16,64,128]{2,1,0:T(8,128)}), f32[16,64,128]{2,1,0:T(8,128)S(1)}, u32[]{:S(2)}, u32[]{:S(2)}) async-start(f32[16,64,128]{2,1,0:T(8,128)} %broadcast_select_fusion.3), calls=%async_computation | async-start | bytes 1048576 | tf_op jit(solution)/shard_map/all_to_all | solution.py:213
  67.5 17.2 %copy-start.15 = (pred[16]{0:T(512)(128)(4,1)}, pred[16]{0:T(512)(128)(4,1)S(1)}, u32[]{:S(2)}) copy-start(pred[16]{0:T(512)(128)(4,1)S(1)} %get-tuple-element.740) | copy-start | bytes 52
  80.2 2.3 copy-start.4
  81.3 2.3 copy-start.21
  86.1 9.4 %copy-start.20 = (s32[16]{0:T(128)S(1)}, s32[16]{0:T(128)}, u32[]{:S(2)}) copy-start(s32[16]{0:T(128)} %param.37) | copy-start | bytes 196
  86.1 39.4 %all-to-all-start.1 = ((f32[64,16,320]{2,0,1:T(8,128)}), f32[64,16,320]{2,0,1:T(8,128)S(1)}, u32[]{:S(2)}, u32[]{:S(2)}) async-start(f32[64,16,320]{2,0,1:T(8,128)} %select_bitcast_fusion.1), calls=%async_computation.1 | async-start | bytes 3145728 | tf_op jit(solution)/shard_map/all_to_all | solution.py:228
  95.5 34.8 %copy-start.11 = (pred[128]{0:T(512)(128)(4,1)}, pred[128]{0:T(512)(128)(4,1)S(1)}, u32[]{:S(2)}) copy-start(pred[128]{0:T(512)(128)(4,1)S(1)} %get-tuple-element.738) | copy-start | bytes 388
  95.6 30.6 %copy-start.17 = (pred[16]{0:T(512)(128)(4,1)}, pred[16]{0:T(512)(128)(4,1)S(1)}, u32[]{:S(2)}) copy-start(pred[16]{0:T(512)(128)(4,1)S(1)} %compare_and_fusion.2) | copy-start | bytes 52
  130.3 2.0 copy-start.7
  130.6 3.2 %copy-start.2 = (f32[1024]{0:T(1024)S(1)}, f32[1024]{0:T(1024)}, u32[]{:S(2)}) copy-start(f32[1024]{0:T(1024)} %get-tuple-element.1287) | copy-start | bytes 12292
  172.1 8.5 %copy-start.14 = (s32[16]{0:T(128)S(1)}, s32[16]{0:T(128)}, u32[]{:S(2)}) copy-start(s32[16]{0:T(128)} %get-tuple-element.652) | copy-start | bytes 196
  173.6 20.8 %copy-start.6 = (f32[320,128,1]{1,0,2:T(8,128)S(1)}, f32[320,128,1]{1,0,2:T(8,128)}, u32[]{:S(2)}) copy-start(f32[320,128,1]{1,0,2:T(8,128)} %constant.252) | copy-start | bytes 491524
  173.6 19.0 %all-to-all-start.2 = ((f32[16,64,128]{2,1,0:T(8,128)}), f32[16,64,128]{2,1,0:T(8,128)S(1)}, u32[]{:S(2)}, u32[]{:S(2)}) async-start(f32[16,64,128]{2,1,0:T(8,128)} %broadcast_select_fusion.2), calls=%async_computation.2 | async-start | bytes 1048576 | tf_op jit(solution)/shard_map/all_to_all | solution.py:213
  194.4 2.2 copy-start.22
  197.1 0.7 copy-start.16
  199.2 39.3 %all-to-all-start.3 = ((f32[64,16,320]{2,0,1:T(8,128)}), f32[64,16,320]{2,0,1:T(8,128)S(1)}, u32[]{:S(2)}, u32[]{:S(2)}) async-start(f32[64,16,320]{2,0,1:T(8,128)} %select_bitcast_fusion), calls=%async_computation.3 | async-start | bytes 3145728 | tf_op jit(solution)/shard_map/all_to_all | solution.py:228
  238.5 0.7 copy-start.18
  242.4 0.8 copy-start.12
  243.2 2.0 copy-start.8
  264.0 0.8 copy-start
where the time goes:
time: 270 us; the launch traced here: 265 us
  waiting for transfers between devices  84.3 us (31%)
  starting transfers between devices  63.1 us (23%)
  other arithmetic  52 us (19%)
  local copies, waits for them, and re-layouts  31.1 us (12%)
  matrix products  23.1 us (9%)
  between operations  6.52 us (2%)
  loops' own time  4.63 us (2%)
    all_to_all x2, waiting for transfers between devices, give_back(): lax.all_to_all(picked, 'grid', split_axis=1, concat_axis=0, tiled=True)  61.5 us
    all_to_all x2, starting transfers between devices, combine(): lax.all_to_all(outgoing, 'grid', split_axis=0, concat_axis=0, tiled=True)  50.1 us
    add x26, other arithmetic, one_substep(): return current + dt_sub * (diffusivity * spread - transport)  26.8 us
    all_to_all x2, waiting for transfers between devices, combine(): lax.all_to_all(outgoing, 'grid', split_axis=0, concat_axis=0, tiled=True)  22.8 us
    all_to_all x2, starting transfers between devices, give_back(): lax.all_to_all(picked, 'grid', split_axis=1, concat_axis=0, tiled=True)  13 us
    slice x52, local copies, waits for them, and re-layouts, one_substep(): jnp.roll(current, 1, axis=1)  10.5 us
    add x26, other arithmetic, one_substep(): jnp.roll(cube_view, 1, axis=0) + jnp.roll(cube_view, -1, axis=0)  6.84 us
  transfers between devices with their start and end apart: 4, of which 4 were waited for; matrix products, arithmetic and copies ran while one was open for 1% of the time, Pallas kernels for 0%

commit v1 on v0

v1 whole, which is shorter than its diff:
```python
import functools

import jax
import jax.numpy as jnp
import numpy as np
from jax import lax
from jax.experimental import pallas as pl
from jax.experimental.pallas import tpu as pltpu
from jax.sharding import PartitionSpec as P

LMIN = 2
NLEV = 4
CLEV = 5
STEPS = 2
SIDE = 2**CLEV
ROW_BITS = 2 * LMIN + NLEV - 1
LANES = 2**ROW_BITS

time_step = 0.02
diffusivity = 0.0024
MESH = pl.DeviceIdType.MESH
VMEM_SPEC = pl.BlockSpec(memory_space=pltpu.VMEM)
SMEM_SPEC = pl.BlockSpec(memory_space=pltpu.SMEM)


def hier_line(line_level):
    points = 2**line_level
    matrix = np.zeros((points, points))
    matrix[0, 0] = 1.0
    for tier_rank in range(1, line_level + 1):
        stride = 2 ** (line_level - tier_rank)
        for entry_at in range(2 ** (tier_rank - 1), 2**tier_rank):
            node_at = (2 * (entry_at - 2 ** (tier_rank - 1)) + 1) * stride
            matrix[entry_at, node_at] += 1.0
            matrix[entry_at, (node_at - stride) % points] -= 0.5
            matrix[entry_at, (node_at + stride) % points] -= 0.5
    return matrix


def dehier_line(line_level):
    points = 2**line_level
    matrix = np.zeros((points, points))
    matrix[0, 0] = 1.0
    for tier_rank in range(1, line_level + 1):
        stride = 2 ** (line_level - tier_rank)
        for entry_at in range(2 ** (tier_rank - 1), 2**tier_rank):
            node_at = (2 * (entry_at - 2 ** (tier_rank - 1)) + 1) * stride
            matrix[node_at] = 0.5 * (
                matrix[(node_at - stride) % points] + matrix[(node_at + stride) % points]
            )
            matrix[node_at, entry_at] += 1.0
    return matrix


def row_tables():
    starts, widths, offsets = ([], [], [])
    running = 0
    for piece_level in range(LMIN, LMIN + NLEV):
        first_row = 0 if piece_level == LMIN else 2 ** (piece_level - 1)
        breadth = 2**LMIN if piece_level == LMIN else 2 ** (piece_level - 1)
        starts.append(first_row)
        widths.append(breadth)
        offsets.append(running)
        running += breadth * 2 ** (ROW_BITS - piece_level)
    padded = -(-running // 128) * 128
    forward, backward, embeds = ([], [], [])
    for shift_level in range(NLEV):
        first_level = LMIN + shift_level
        second_level = ROW_BITS - first_level
        tensor = np.kron(hier_line(first_level), hier_line(second_level))
        inverse = np.kron(dehier_line(first_level), dehier_line(second_level))
        order_list, place_list = ([], [])
        for slot_index in range(shift_level + 1):
            for second in range(2**second_level):
                for first_idx in range(starts[slot_index], starts[slot_index] + widths[slot_index]):
                    order_list.append(first_idx * 2**second_level + second)
                    place_list.append(
                        offsets[slot_index]
                        + second * widths[slot_index]
                        + first_idx
                        - starts[slot_index]
                    )
        embedding = np.zeros((padded, LANES))
        embedding[np.array(place_list), np.arange(LANES)] = 1.0
        forward.append(tensor[order_list].T)
        backward.append(inverse[:, order_list].T)
        embeds.append(embedding)
    stacked = np.concatenate([e.T for e in embeds], axis=0)
    cover = np.stack([e.sum(axis=1) for e in embeds])
    return np.stack(forward), np.stack(backward), stacked, cover, running, padded


def tiers():
    found = []
    for tier_rank in range(1, CLEV + 1):
        stride = 2 ** (CLEV - tier_rank)
        for entry_at in range(2 ** (tier_rank - 1), 2**tier_rank):
            node_at = (2 * (entry_at - 2 ** (tier_rank - 1)) + 1) * stride
            found.append((entry_at, node_at, node_at - stride, (node_at + stride) % SIDE))
    return found


def split_dot(values, matrix):
    high = values.astype(jnp.bfloat16)
    low = (values - high.astype(jnp.float32)).astype(jnp.bfloat16)
    return jnp.dot(high, matrix, preferred_element_type=jnp.float32) + jnp.dot(
        low, matrix, preferred_element_type=jnp.float32
    )


def hier_lines(read, write):
    vals = [read(i) for i in range(SIDE)]
    write(0, vals[0])
    for entry_at, node_at, low_at, high_at in tiers():
        write(entry_at, vals[node_at] - 0.5 * (vals[low_at] + vals[high_at]))


def dehier_lines(read, write):
    vals = [None] * SIDE
    vals[0] = read(0)
    write(0, vals[0])
    for entry_at, node_at, low_at, high_at in tiers():
        vals[node_at] = read(entry_at) + 0.5 * (vals[low_at] + vals[high_at])
        write(node_at, vals[node_at])


def lines_first(op, buf, src, dst):
    for part in range(SIDE // 8):
        op(
            lambda i: buf[pl.ds(src + i * SIDE + part * 8, 8), :],
            lambda i, v: buf.__setitem__((pl.ds(dst + i * SIDE + part * 8, 8), slice(None)), v),
        )


def lines_second(op, buf, src, dst):
    for part in range(SIDE // 8):
        op(
            lambda i: buf[pl.ds(src + part * 8 * SIDE + i, 8, stride=SIDE), :],
            lambda i, v: buf.__setitem__(
                (pl.ds(dst + part * 8 * SIDE + i, 8, stride=SIDE), slice(None)), v
            ),
        )


def local_kernel(
    count, pre, post, in_map, out_map, tables, devices,
    levels, coeffs, assign, assign_next, owner, row_speed, x_ref, col_ref, *rest,
):
    rest = list(rest)
    back_ref = rest.pop(0) if pre else None
    fwd_ref = rest.pop(0) if post else None
    out_ref = rest.pop(0)
    tab_ref = rest.pop(0) if tables else None
    buf, plus, minus = rest
    cells = SIDE * SIDE
    block = cells // devices
    sections = devices // NLEV
    me = lax.axis_index("grid")

    if tables:
        def fill(g, carry):
            slot = (levels[g] - LMIN) * sections + g // NLEV
            tab_ref[slot] = assign[g]
            tab_ref[devices + slot] = assign_next[g]
            tab_ref[2 * devices + assign_next[g]] = slot
            tab_ref[3 * devices + slot] = coeffs[g]
            return carry
        lax.fori_loop(0, devices, fill, 0)

    own = lax.fori_loop(
        0, devices, lambda g, seen: jnp.where(assign[g] == me, g, seen), jnp.int32(0)
    )
    level = levels[own]
    inner = jnp.left_shift(jnp.int32(1), ROW_BITS - level)
    refine = jnp.left_shift(jnp.int32(1), level - LMIN)
    scale_one = jnp.left_shift(jnp.int32(1), level).astype(jnp.float32)
    scale_two = inner.astype(jnp.float32)
    dt = jnp.float32(time_step)
    for shift in range(1, NLEV):
        dt = jnp.where(level == LMIN + shift, jnp.float32(time_step / 2**shift), dt)
    k1 = dt * diffusivity * scale_one * scale_one
    k2 = dt * diffusivity * scale_two * scale_two
    k3 = dt * diffusivity * float(4**CLEV)
    k0 = 1.0 - 2.0 * k1 - 2.0 * k2 - 4.0 * k3

    lane = lax.broadcasted_iota(jnp.int32, (8, LANES), 1)
    inner_pos = jnp.bitwise_and(lane, inner - 1)
    sample_at = inner_pos * jnp.left_shift(jnp.int32(1), level - LMIN)
    row_factor = jnp.zeros((8, LANES), jnp.float32)
    for f in range(row_speed.shape[0]):
        row_factor = jnp.where(sample_at == f, row_speed[f], row_factor)
    row_factor = row_factor * (dt * 0.5 * scale_one)

    def speeds(i, carry):
        at = pl.multiple_of(i * 32, 32)
        vel = col_ref[pl.ds(at, 32), :] * jnp.concatenate([row_factor] * 4, axis=0)
        plus[pl.ds(at, 32), :] = k1 - vel
        minus[pl.ds(at, 32), :] = k1 + vel
        return carry
    lax.fori_loop(0, cells // 32, speeds, 0)

    if pre:
        def take(b, carry):
            buf[pl.ds(pl.multiple_of(b * block, block), block), :] = x_ref[owner[b] if in_map else b]
            return carry
        lax.fori_loop(0, devices, take, 0)
        weights = back_ref[level - LMIN]
        for at in range(0, cells, 256):
            buf[pl.ds(cells + at, 256), :] = split_dot(buf[pl.ds(at, 256), :], weights)
        lines_first(dehier_lines, buf, cells, 0)
        lines_second(dehier_lines, buf, 0, cells)
        start = 1
    else:
        buf[pl.ds(0, cells), :] = x_ref[0]
        start = 0

    pos_slab = jnp.concatenate([inner_pos] * 4, axis=0)
    at_first = pos_slab == 0
    at_last = pos_slab == inner - 1
    group = 4

    def substep(turn, parity):
        src = parity * cells
        dst = (1 - parity) * cells

        def slabs(i, carry):
            base = i * group
            cur = []
            for j in range(-1, group + 1):
                m = jnp.bitwise_and(base + j, SIDE - 1)
                cur.append(buf[pl.ds(pl.multiple_of(src + m * SIDE, SIDE), SIDE), :])
            for j in range(group):
                u = cur[j + 1]
                up1 = pltpu.roll(u, LANES - inner, 1)
                dn1 = pltpu.roll(u, inner, 1)
                up2 = pltpu.roll(jnp.where(at_first, dn1, u), LANES - 1, 1)
                dn2 = pltpu.roll(jnp.where(at_last, up1, u), 1, 1)
                side = (pltpu.roll(u, 1, 0) + pltpu.roll(u, SIDE - 1, 0)) + (cur[j] + cur[j + 2])
                at = pl.multiple_of((base + j) * SIDE, SIDE)
                new = k0 * u + plus[pl.ds(at, SIDE), :] * up1
                new = new + minus[pl.ds(at, SIDE), :] * dn1
                new = new + (k2 * (up2 + dn2) + k3 * side)
                buf[pl.ds(pl.multiple_of(dst + (base + j) * SIDE, SIDE), SIDE), :] = new
            return carry

        lax.fori_loop(0, SIDE // group, slabs, 0)
        return 1 - parity

    final = lax.fori_loop(0, refine * count, substep, jnp.int32(start))

    if post:
        src, dst = start * cells, (1 - start) * cells
        lines_first(hier_lines, buf, src, dst)
        lines_second(hier_lines, buf, dst, src)
        weight = coeffs[own].astype(jnp.float32)
        weights = fwd_ref[level - LMIN]
        for at in range(0, cells, 256):
            buf[pl.ds(dst + at, 256), :] = weight * split_dot(buf[pl.ds(src + at, 256), :], weights)

        def give(b, carry):
            out_ref[owner[b] if out_map else b] = buf[
                pl.ds(pl.multiple_of(dst + b * block, block), block), :
            ]
            return carry
        lax.fori_loop(0, devices, give, 0)
    else:
        out_ref[0] = buf[pl.ds(pl.multiple_of(final * cells, cells), cells), :]


def exchange_kernel(
    source_row, keep, devices, tab, x_ref, embed_ref, take_ref, cover_ref, out_ref, *rest
):
    rest = list(rest)
    keep_ref = rest.pop(0) if keep else None
    recv, wide, packs, send2, sems = rest
    block = x_ref.shape[1]
    sections = devices // NLEV
    padded = cover_ref.shape[1]
    me = lax.axis_index("grid")

    barrier = pltpu.get_barrier_semaphore()

    def greet(i, carry):
        pl.semaphore_signal(
            barrier, inc=1, device_id={"grid": lax.rem(me + i, devices)}, device_id_type=MESH
        )
        return carry

    lax.fori_loop(1, devices, greet, 0)
    pl.semaphore_wait(barrier, devices - 1)

    def copy_of(src, dst, base, i):
        to = lax.rem(me + i, devices)
        return pltpu.make_async_remote_copy(
            src_ref=src.at[to],
            dst_ref=dst.at[me],
            send_sem=sems.at[base, i],
            recv_sem=sems.at[base + 1, i],
            device_id={"grid": to},
            device_id_type=MESH,
        )

    def start_first(i, carry):
        copy_of(x_ref, recv, 0, i).start()
        return carry

    lax.fori_loop(1, devices, start_first, 0)
    recv[me] = x_ref[me]

    def wait_first(i, carry):
        copy_of(x_ref, recv, 0, i).wait()
        return carry

    lax.fori_loop(1, devices, wait_first, 0)

    def gather(q, carry):
        for lev in range(NLEV):
            wide[pl.ds(pl.multiple_of(q * block, block), block), lev * LANES : (lev + 1) * LANES] = recv[
                tab[source_row * devices + lev * sections + q]
            ]
        return carry

    lax.fori_loop(0, sections, gather, 0)
    total = split_dot(wide[...], embed_ref[...])
    wide[:, 0:padded] = total

    def divide(q, carry):
        denom = jnp.zeros((1, padded), jnp.float32)
        for lev in range(NLEV):
            denom = denom + cover_ref[lev : lev + 1, :] * tab[
                3 * devices + lev * sections + q
            ].astype(jnp.float32)
        inverse = 1.0 / jnp.where(denom > 0.0, denom, 1.0)
        at = pl.multiple_of(q * block, block)
        value = wide[pl.ds(at, block), 0:padded] * inverse
        wide[pl.ds(at, block), 0:padded] = value
        if keep:
            keep_ref[q] = value
        return carry

    lax.fori_loop(0, sections, divide, 0)
    picked = split_dot(wide[:, 0:padded], take_ref[...])
    for lev in range(NLEV):
        packs[pl.ds(lev * sections, sections)] = picked[:, lev * LANES : (lev + 1) * LANES].reshape(
            sections, block, LANES
        )

    def start_second(i, carry):
        to = lax.rem(me + i, devices)
        send2[to] = packs[tab[2 * devices + to]]
        copy_of(send2, out_ref, 2, i).start()
        return carry

    lax.fori_loop(1, devices, start_second, 0)
    out_ref[me] = packs[tab[2 * devices + me]]

    def wait_second(i, carry):
        copy_of(send2, out_ref, 2, i).wait()
        return carry

    lax.fori_loop(1, devices, wait_second, 0)


def local(start_field, col_speed, row_speed, levels, coeffs, assign_first, assign_second, owner_of):
    forward, backward, stacked, cover, section_rows, padded = row_tables()
    forward = jnp.asarray(forward, jnp.bfloat16)
    backward = jnp.asarray(backward, jnp.bfloat16)
    embed = jnp.asarray(stacked, jnp.bfloat16)
    take = jnp.asarray(stacked.T, jnp.bfloat16)
    cover = jnp.asarray(cover, jnp.float32)
    devices = lax.axis_size("grid")
    cells, lanes = start_field.shape[1:]
    block = cells // devices
    sections = devices // NLEV
    columns = jnp.broadcast_to(col_speed[:, None], (cells, lanes))

    def stage(x, assign, assign_next, count, pre, post, in_map, out_map, tables):
        args = [levels, coeffs, assign, assign_next, owner_of, row_speed, x, columns]
        specs = [SMEM_SPEC] * 6 + [VMEM_SPEC] * 2
        if pre:
            args.append(backward)
            specs.append(VMEM_SPEC)
        if post:
            args.append(forward)
            specs.append(VMEM_SPEC)
        shape = (devices, block, lanes) if post else (1, cells, lanes)
        outs = [jax.ShapeDtypeStruct(shape, jnp.float32)]
        out_specs = [VMEM_SPEC]
        if tables:
            outs.append(jax.ShapeDtypeStruct((4 * devices,), jnp.int32))
            out_specs.append(SMEM_SPEC)
        return pl.pallas_call(
            functools.partial(local_kernel, count, pre, post, in_map, out_map, tables, devices),
            out_shape=outs,
            in_specs=specs,
            out_specs=out_specs,
            scratch_shapes=[
                pltpu.VMEM((2 * cells, lanes), jnp.float32),
                pltpu.VMEM((cells, lanes), jnp.float32),
                pltpu.VMEM((cells, lanes), jnp.float32),
            ],
        )(*args)

    def exchange(x, tab, source_row, keep, collective_id):
        outs = [jax.ShapeDtypeStruct((devices, block, lanes), jnp.float32)]
        if keep:
            outs.append(jax.ShapeDtypeStruct((sections, block, padded), jnp.float32))
        return pl.pallas_call(
            functools.partial(exchange_kernel, source_row, keep, devices),
            out_shape=outs,
            in_specs=[SMEM_SPEC] + [VMEM_SPEC] * 4,
            out_specs=[VMEM_SPEC] * len(outs),
            scratch_shapes=[
                pltpu.VMEM((devices, block, lanes), jnp.float32),
                pltpu.VMEM((sections * block, NLEV * lanes), jnp.float32),
                pltpu.VMEM((devices, block, lanes), jnp.float32),
                pltpu.VMEM((devices, block, lanes), jnp.float32),
                pltpu.SemaphoreType.DMA((4, devices)),
            ],
            compiler_params=pltpu.CompilerParams(
                collective_id=collective_id, has_side_effects=True
            ),
        )(tab, x, embed, take, cover)

    outgoing, tab = stage(
        start_field, assign_first, assign_second, STEPS, False, True, False, False, True
    )
    (restricted,) = exchange(outgoing, tab, 0, False, 0)
    (outgoing,) = stage(
        restricted, assign_second, assign_second, STEPS, True, True, False, True, False
    )
    restricted, kept = exchange(outgoing, tab, 1, True, 1)
    (final,) = stage(restricted, assign_second, assign_second, 1, True, False, True, False, False)
    combined = jnp.transpose(kept[:, :, :section_rows], (1, 0, 2)).reshape(
        block, sections * section_rows
    )
    return combined, final


def solution(mesh):
    placed = (
        P(("groups", "grid"), None, None),
        P(),
        P(),
        P("groups"),
        P("groups"),
        P("groups"),
        P("groups"),
        P("groups"),
    )
    return jax.shard_map(
        local,
        mesh=mesh,
        in_specs=placed,
        out_specs=(P(("groups", "grid"), None), P(("groups", "grid"), None, None)),
        check_vma=False,
    )
```

time: 270 us -> 137 us (0.51)
  the two profiles are of different devices: /device:TPU:24 before, /device:TPU:10 now
where the time goes in v1:
time: 137 us; the launch traced here: 135 us
  Pallas kernels  131 us (96%)
  local copies, waits for them, and re-layouts  3.95 us (3%)
    pallas_call x2, Pallas kernels, exchange(): pl.pallas_call(functools.partial(exchange_kernel, source_row, keep, devic...  82.2 us
    pallas_call x3, Pallas kernels, stage(): pl.pallas_call(functools.partial(local_kernel, count, pre, post, in_map,...  48.5 us

profile of v1, /device:TPU:10, one launch (start us, length us, event | category | flops | bytes accessed | tf_op | source)
XLA Modules:
  0.0 135.3 jit_solution(14466259584388774591)
XLA Ops:
  0.6 1.7 %broadcast_in_dim.2.col_ref = f32[1024,128]{1,0:T(8,128)} broadcast(f32[1024]{0:T(1024)} %param.14), dimensions={0} | broadcast | bytes 528384 | tf_op jit(solution)/shard_map/broadcast_in_dim | solution.py:375
  2.3 6.5 %shard_map.140 = (f32[16,64,128]{2,1,0:T(8,128)}, s32[64]{0:T(128)}) custom-call(s32[16]{0:T(128)} %levels.5, s32[16]{0:T(128)} %coeffs.5, s32[16]{0:T(128)} %assign.3, s32[16]{0:T(128)} %assign_next.5, s32[16]{0:T(128)} %owner.5, f32[32]{0:T(128)} %row_speed.5, f32[1,1024,128]{2,1,0:T(8,128)} %x_ref.1, f32[1024,128]{1,0:T(8,128)} %broadcast_in_dim.2.col_ref, ...), custom_call_target="tpu_custom_call" | custom-call | tf_op jit(solution)/shard_map/pallas_call | solution.py:392
  8.8 49.6 %shard_map.141.x_ref = f32[16,64,128]{2,1,0:T(8,128)} custom-call(s32[64]{0:T(128)} %get-tuple-element.6.tab, f32[16,64,128]{2,1,0:T(8,128)} %get-tuple-element.7.x_ref, bf16[512,384]{1,0:T(8,128)(2,1)} %constant.12.clone.embed_ref, bf16[384,512]{1,0:T(8,128)(2,1)} %constant.13.clone.take_ref, f32[4,384]{1,0:T(4,128)} %constant.14.clone.cover_ref), custom_call_target="tpu_custom_call" | custom-call | tf_op jit(solution)/shard_map/pallas_call | solution.py:408
  58.4 27.2 %shard_map.142.x_ref = f32[16,64,128]{2,1,0:T(8,128)} custom-call(s32[16]{0:T(128)} %levels.5, s32[16]{0:T(128)} %coeffs.5, s32[16]{0:T(128)} %assign_next.5, s32[16]{0:T(128)} %assign_next.5, s32[16]{0:T(128)} %owner.5, f32[32]{0:T(128)} %row_speed.5, f32[16,64,128]{2,1,0:T(8,128)} %shard_map.141.x_ref, f32[1024,128]{1,0:T(8,128)} %broadcast_in_dim.2.col_ref, ...), custom_call_target="tpu_custom_call" | custom-call | tf_op jit(solution)/shard_map/pallas_call | solution.py:392
  85.6 32.5 %shard_map.143 = (f32[16,64,128]{2,1,0:T(8,128)}, f32[4,64,384]{2,1,0:T(8,128)}) custom-call(s32[64]{0:T(128)} %get-tuple-element.6.tab, f32[16,64,128]{2,1,0:T(8,128)} %shard_map.142.x_ref, bf16[512,384]{1,0:T(8,128)(2,1)} %constant.12.clone.embed_ref, bf16[384,512]{1,0:T(8,128)(2,1)} %constant.13.clone.take_ref, f32[4,384]{1,0:T(4,128)} %constant.14.clone.cover_ref), custom_call_target="tpu_custom_call" | custom-call | tf_op jit(solution)/shard_map/pallas_call | solution.py:408
  118.2 1.0 slice_bitcast_fusion
  119.2 0.3 copy.15
  119.5 1.0 reshape.8
  120.5 14.8 %shard_map.144 = f32[1,1024,128]{2,1,0:T(8,128)} custom-call(s32[16]{0:T(128)} %levels.5, s32[16]{0:T(128)} %coeffs.5, s32[16]{0:T(128)} %assign_next.5, s32[16]{0:T(128)} %assign_next.5, s32[16]{0:T(128)} %owner.5, f32[32]{0:T(128)} %row_speed.5, f32[16,64,128]{2,1,0:T(8,128)} %get-tuple-element.9.x_ref, f32[1024,128]{1,0:T(8,128)} %broadcast_in_dim.2.col_ref, ...), custom_call_target="tpu_custom_call" | custom-call | tf_op jit(solution)/shard_map/pallas_call | solution.py:392

commit v2 on v1

--- a/solution.py
+++ b/solution.py
@@ -90,6 +90,24 @@
     return np.stack(forward), np.stack(backward), stacked, cover, running, padded
 
 
+def stencil_tables():
+    tables = []
+    for first_level in range(LMIN, LMIN + NLEV):
+        inner = 2 ** (ROW_BITS - first_level)
+        both = np.zeros((LANES, 2 * LANES))
+        for row in range(LANES):
+            base, pos = row - row % inner, row % inner
+            both[row, row] -= 2.0 * (4**first_level + inner * inner)
+            for sign in (1, -1):
+                far = (row + sign * inner) % LANES
+                near = base + (pos + sign) % inner
+                both[far, row] += 4**first_level
+                both[near, row] += inner * inner
+                both[far, LANES + row] += sign
+        tables.append(np.concatenate([both, both], axis=0))
+    return np.stack(tables)
+
+
 def tiers():
     found = []
     for tier_rank in range(1, CLEV + 1):
@@ -144,14 +162,14 @@
 
 def local_kernel(
     count, pre, post, in_map, out_map, tables, devices,
-    levels, coeffs, assign, assign_next, owner, row_speed, x_ref, col_ref, *rest,
+    levels, coeffs, assign, assign_next, owner, row_speed, x_ref, col_ref, stencil_ref, *rest,
 ):
     rest = list(rest)
     back_ref = rest.pop(0) if pre else None
     fwd_ref = rest.pop(0) if post else None
     out_ref = rest.pop(0)
     tab_ref = rest.pop(0) if tables else None
-    buf, plus, minus = rest
+    buf, speed = rest
     cells = SIDE * SIDE
     block = cells // devices
     sections = devices // NLEV
@@ -174,14 +192,12 @@
     inner = jnp.left_shift(jnp.int32(1), ROW_BITS - level)
     refine = jnp.left_shift(jnp.int32(1), level - LMIN)
     scale_one = jnp.left_shift(jnp.int32(1), level).astype(jnp.float32)
-    scale_two = inner.astype(jnp.float32)
     dt = jnp.float32(time_step)
     for shift in range(1, NLEV):
         dt = jnp.where(level == LMIN + shift, jnp.float32(time_step / 2**shift), dt)
-    k1 = dt * diffusivity * scale_one * scale_one
-    k2 = dt * diffusivity * scale_two * scale_two
+    k1 = dt * diffusivity
     k3 = dt * diffusivity * float(4**CLEV)
-    k0 = 1.0 - 2.0 * k1 - 2.0 * k2 - 4.0 * k3
+    k0 = 1.0 - 4.0 * k3
 
     lane = lax.broadcasted_iota(jnp.int32, (8, LANES), 1)
     inner_pos = jnp.bitwise_and(lane, inner - 1)
@@ -193,9 +209,7 @@
 
     def speeds(i, carry):
         at = pl.multiple_of(i * 32, 32)
-        vel = col_ref[pl.ds(at, 32), :] * jnp.concatenate([row_factor] * 4, axis=0)
-        plus[pl.ds(at, 32), :] = k1 - vel
-        minus[pl.ds(at, 32), :] = k1 + vel
+        speed[pl.ds(at, 32), :] = col_ref[pl.ds(at, 32), :] * jnp.concatenate([row_factor] * 4, axis=0)
         return carry
     lax.fori_loop(0, cells // 32, speeds, 0)
 
@@ -214,10 +228,8 @@
         buf[pl.ds(0, cells), :] = x_ref[0]
         start = 0
 
-    pos_slab = jnp.concatenate([inner_pos] * 4, axis=0)
-    at_first = pos_slab == 0
-    at_last = pos_slab == inner - 1
-    group = 4
+    group = 8
+    rows = group * SIDE
 
     def substep(turn, parity):
         src = parity * cells
@@ -225,21 +237,25 @@
 
         def slabs(i, carry):
             base = i * group
+            at = pl.multiple_of(i * rows, rows)
+            chunk = buf[pl.ds(pl.multiple_of(src + at, rows), rows), :]
+            high = chunk.astype(jnp.bfloat16)
+            low = (chunk - high.astype(jnp.float32)).astype(jnp.bfloat16)
+            mixed = jnp.dot(
+                jnp.concatenate([high, low], axis=1),
+                stencil_ref[level - LMIN],
+                preferred_element_type=jnp.float32,
+            )
             cur = []
             for j in range(-1, group + 1):
                 m = jnp.bitwise_and(base + j, SIDE - 1)
                 cur.append(buf[pl.ds(pl.multiple_of(src + m * SIDE, SIDE), SIDE), :])
             for j in range(group):
                 u = cur[j + 1]
-                up1 = pltpu.roll(u, LANES - inner, 1)
-                dn1 = pltpu.roll(u, inner, 1)
-                up2 = pltpu.roll(jnp.where(at_first, dn1, u), LANES - 1, 1)
-                dn2 = pltpu.roll(jnp.where(at_last, up1, u), 1, 1)
                 side = (pltpu.roll(u, 1, 0) + pltpu.roll(u, SIDE - 1, 0)) + (cur[j] + cur[j + 2])
-                at = pl.multiple_of((base + j) * SIDE, SIDE)
-                new = k0 * u + plus[pl.ds(at, SIDE), :] * up1
-                new = new + minus[pl.ds(at, SIDE), :] * dn1
-                new = new + (k2 * (up2 + dn2) + k3 * side)
+                here = slice(j * SIDE, (j + 1) * SIDE)
+                new = (k0 * u + k3 * side) + k1 * mixed[here, :LANES]
+                new = new - speed[pl.ds(at + j * SIDE, SIDE), :] * mixed[here, LANES:]
                 buf[pl.ds(pl.multiple_of(dst + (base + j) * SIDE, SIDE), SIDE), :] = new
             return carry
 
@@ -289,6 +305,9 @@
     lax.fori_loop(1, devices, greet, 0)
     pl.semaphore_wait(barrier, devices - 1)
 
+    def far_first(k):
+        return lax.rem(k + devices // 2 - 1, devices - 1) + 1
+
     def copy_of(src, dst, base, i):
         to = lax.rem(me + i, devices)
         return pltpu.make_async_remote_copy(
@@ -300,11 +319,12 @@
             device_id_type=MESH,
         )
 
-    def start_first(i, carry):
+    def start_first(k, carry):
+        i = far_first(k)
         copy_of(x_ref, recv, 0, i).start()
         return carry
 
-    lax.fori_loop(1, devices, start_first, 0)
+    lax.fori_loop(0, devices - 1, start_first, 0)
     recv[me] = x_ref[me]
 
     def wait_first(i, carry):
@@ -345,13 +365,14 @@
             sections, block, LANES
         )
 
-    def start_second(i, carry):
+    def start_second(k, carry):
+        i = far_first(k)
         to = lax.rem(me + i, devices)
         send2[to] = packs[tab[2 * devices + to]]
         copy_of(send2, out_ref, 2, i).start()
         return carry
 
-    lax.fori_loop(1, devices, start_second, 0)
+    lax.fori_loop(0, devices - 1, start_second, 0)
     out_ref[me] = packs[tab[2 * devices + me]]
 
     def wait_second(i, carry):
@@ -368,6 +389,7 @@
     embed = jnp.asarray(stacked, jnp.bfloat16)
     take = jnp.asarray(stacked.T, jnp.bfloat16)
     cover = jnp.asarray(cover, jnp.float32)
+    stencils = jnp.asarray(stencil_tables(), jnp.bfloat16)
     devices = lax.axis_size("grid")
     cells, lanes = start_field.shape[1:]
     block = cells // devices
@@ -375,8 +397,8 @@
     columns = jnp.broadcast_to(col_speed[:, None], (cells, lanes))
 
     def stage(x, assign, assign_next, count, pre, post, in_map, out_map, tables):
-        args = [levels, coeffs, assign, assign_next, owner_of, row_speed, x, columns]
-        specs = [SMEM_SPEC] * 6 + [VMEM_SPEC] * 2
+        args = [levels, coeffs, assign, assign_next, owner_of, row_speed, x, columns, stencils]
+        specs = [SMEM_SPEC] * 6 + [VMEM_SPEC] * 3
         if pre:
             args.append(backward)
             specs.append(VMEM_SPEC)
@@ -397,7 +419,6 @@
             scratch_shapes=[
                 pltpu.VMEM((2 * cells, lanes), jnp.float32),
                 pltpu.VMEM((cells, lanes), jnp.float32),
-                pltpu.VMEM((cells, lanes), jnp.float32),
             ],
         )(*args)
 

time: 137 us -> 112 us (0.82)
  the two profiles are of different devices: /device:TPU:10 before, /device:TPU:1 now
where the time goes in v2:
time: 112 us; the launch traced here: 114 us
  Pallas kernels  110 us (98%)
  local copies, waits for them, and re-layouts  3.95 us (4%)
    pallas_call x2, Pallas kernels, exchange(): pl.pallas_call(functools.partial(exchange_kernel, source_row, keep, devic...  66.5 us
    pallas_call x3, Pallas kernels, stage(): pl.pallas_call(functools.partial(local_kernel, count, pre, post, in_map,...  43.2 us

profile of v2, /device:TPU:1, one launch (start us, length us, event | category | flops | bytes accessed | tf_op | source)
XLA Modules:
  0.0 114.3 jit_solution(6253978441098835414)
XLA Ops:
  0.6 1.7 %broadcast_in_dim.2.col_ref = f32[1024,128]{1,0:T(8,128)} broadcast(f32[1024]{0:T(1024)} %param.15), dimensions={0} | broadcast | bytes 528384 | tf_op jit(solution)/shard_map/broadcast_in_dim | solution.py:397
  2.3 16.2 %shard_map.149 = (f32[16,64,128]{2,1,0:T(8,128)}, s32[64]{0:T(128)}) custom-call(s32[16]{0:T(128)} %levels.5, s32[16]{0:T(128)} %coeffs.5, s32[16]{0:T(128)} %assign.3, s32[16]{0:T(128)} %assign_next.5, s32[16]{0:T(128)} %owner.5, f32[32]{0:T(128)} %row_speed.5, f32[1,1024,128]{2,1,0:T(8,128)} %x_ref.1, f32[1024,128]{1,0:T(8,128)} %broadcast_in_dim.2.col_ref, ...), custom_call_target="tpu_custom_call" | custom-call | tf_op jit(solution)/shard_map/pallas_call | solution.py:414
  18.5 35.0 %shard_map.150.x_ref = f32[16,64,128]{2,1,0:T(8,128)} custom-call(s32[64]{0:T(128)} %get-tuple-element.6.tab, f32[16,64,128]{2,1,0:T(8,128)} %get-tuple-element.7.x_ref, bf16[512,384]{1,0:T(8,128)(2,1)} %constant.14.clone.embed_ref, bf16[384,512]{1,0:T(8,128)(2,1)} %constant.15.clone.take_ref, f32[4,384]{1,0:T(4,128)} %constant.16.clone.cover_ref), custom_call_target="tpu_custom_call" | custom-call | tf_op jit(solution)/shard_map/pallas_call | solution.py:429
  53.5 17.1 %shard_map.151.x_ref = f32[16,64,128]{2,1,0:T(8,128)} custom-call(s32[16]{0:T(128)} %levels.5, s32[16]{0:T(128)} %coeffs.5, s32[16]{0:T(128)} %assign_next.5, s32[16]{0:T(128)} %assign_next.5, s32[16]{0:T(128)} %owner.5, f32[32]{0:T(128)} %row_speed.5, f32[16,64,128]{2,1,0:T(8,128)} %shard_map.150.x_ref, f32[1024,128]{1,0:T(8,128)} %broadcast_in_dim.2.col_ref, ...), custom_call_target="tpu_custom_call" | custom-call | tf_op jit(solution)/shard_map/pallas_call | solution.py:414
  70.6 31.6 %shard_map.152 = (f32[16,64,128]{2,1,0:T(8,128)}, f32[4,64,384]{2,1,0:T(8,128)}) custom-call(s32[64]{0:T(128)} %get-tuple-element.6.tab, f32[16,64,128]{2,1,0:T(8,128)} %shard_map.151.x_ref, bf16[512,384]{1,0:T(8,128)(2,1)} %constant.14.clone.embed_ref, bf16[384,512]{1,0:T(8,128)(2,1)} %constant.15.clone.take_ref, f32[4,384]{1,0:T(4,128)} %constant.16.clone.cover_ref), custom_call_target="tpu_custom_call" | custom-call | tf_op jit(solution)/shard_map/pallas_call | solution.py:429
  102.2 1.0 slice_bitcast_fusion
  103.2 0.3 copy.16
  103.5 1.0 reshape.8
  104.5 9.9 %shard_map.153 = f32[1,1024,128]{2,1,0:T(8,128)} custom-call(s32[16]{0:T(128)} %levels.5, s32[16]{0:T(128)} %coeffs.5, s32[16]{0:T(128)} %assign_next.5, s32[16]{0:T(128)} %assign_next.5, s32[16]{0:T(128)} %owner.5, f32[32]{0:T(128)} %row_speed.5, f32[16,64,128]{2,1,0:T(8,128)} %get-tuple-element.9.x_ref, f32[1024,128]{1,0:T(8,128)} %broadcast_in_dim.2.col_ref, ...), custom_call_target="tpu_custom_call" | custom-call | tf_op jit(solution)/shard_map/pallas_call | solution.py:414

commit v3 on v2

--- a/solution.py
+++ b/solution.py
@@ -284,15 +284,21 @@
 
 
 def exchange_kernel(
-    source_row, keep, devices, tab, x_ref, embed_ref, take_ref, cover_ref, out_ref, *rest
+    source_row, keep, devices, parts, section_rows,
+    tab, x_ref, embed_ref, take_ref, cover_ref, out_ref, *rest,
 ):
     rest = list(rest)
     keep_ref = rest.pop(0) if keep else None
-    recv, wide, packs, send2, sems = rest
+    recvs = rest[:parts]
+    wide, packs, send2, kept, sems = rest[parts:]
     block = x_ref.shape[1]
+    part_cols = block // parts
     sections = devices // NLEV
     padded = cover_ref.shape[1]
     me = lax.axis_index("grid")
+    half = devices // 2
+    my_half = me // half
+    my_place = lax.rem(me, half)
 
     barrier = pltpu.get_barrier_semaphore()
 
@@ -305,81 +311,84 @@
     lax.fori_loop(1, devices, greet, 0)
     pl.semaphore_wait(barrier, devices - 1)
 
-    def far_first(k):
-        return lax.rem(k + devices // 2 - 1, devices - 1) + 1
-
-    def copy_of(src, dst, base, i):
-        to = lax.rem(me + i, devices)
+    def partner(across, j):
+        return lax.rem(my_half + across, 2) * half + lax.rem(my_place + j, half)
+
+    def copy_of(src, dst, phase, part, across, j):
+        to = partner(across, j)
+        cols = slice(part * part_cols, (part + 1) * part_cols)
+        into = dst.at[me] if phase == 0 else dst.at[me, cols]
+        base = 2 * (phase * parts + part)
         return pltpu.make_async_remote_copy(
-            src_ref=src.at[to],
-            dst_ref=dst.at[me],
-            send_sem=sems.at[base, i],
-            recv_sem=sems.at[base + 1, i],
+            src_ref=src.at[to, cols],
+            dst_ref=into,
+            send_sem=sems.at[base, across * half + j],
+            recv_sem=sems.at[base + 1, across * half + j],
             device_id={"grid": to},
             device_id_type=MESH,
         )
 
-    def start_first(k, carry):
-        i = far_first(k)
-        copy_of(x_ref, recv, 0, i).start()
-        return carry
-
-    lax.fori_loop(0, devices - 1, start_first, 0)
-    recv[me] = x_ref[me]
-
-    def wait_first(i, carry):
-        copy_of(x_ref, recv, 0, i).wait()
-        return carry
-
-    lax.fori_loop(1, devices, wait_first, 0)
-
-    def gather(q, carry):
+    def each_partner(act):
+        for across in (1, 0):
+            def body(j, carry, across=across):
+                act(across, j)
+                return carry
+            lax.fori_loop(1 - across, half, body, 0)
+
+    for part in range(parts):
+        each_partner(lambda across, j: copy_of(x_ref, recvs[part], 0, part, across, j).start())
+    for part in range(parts):
+        recvs[part][me] = x_ref[me, part * part_cols : (part + 1) * part_cols]
+
+    for part in range(parts):
+        each_partner(lambda across, j: copy_of(x_ref, recvs[part], 0, part, across, j).wait())
+        cols = slice(part * part_cols, (part + 1) * part_cols)
+
+        def gather(q, carry):
+            at = pl.multiple_of(q * part_cols, part_cols)
+            for lev in range(NLEV):
+                wide[pl.ds(at, part_cols), lev * LANES : (lev + 1) * LANES] = recvs[part][
+                    tab[source_row * devices + lev * sections + q]
+                ]
+            return carry
+
+        lax.fori_loop(0, sections, gather, 0)
+        wide[:, 0:padded] = split_dot(wide[...], embed_ref[...])
+
+        def divide(q, carry):
+            denom = jnp.zeros((1, padded), jnp.float32)
+            for lev in range(NLEV):
+                denom = denom + cover_ref[lev : lev + 1, :] * tab[
+                    3 * devices + lev * sections + q
+                ].astype(jnp.float32)
+            inverse = 1.0 / jnp.where(denom > 0.0, denom, 1.0)
+            at = pl.multiple_of(q * part_cols, part_cols)
+            value = wide[pl.ds(at, part_cols), 0:padded] * inverse
+            wide[pl.ds(at, part_cols), 0:padded] = value
+            if keep:
+                kept[q, cols] = value
+            return carry
+
+        lax.fori_loop(0, sections, divide, 0)
+        picked = split_dot(wide[:, 0:padded], take_ref[...])
         for lev in range(NLEV):
-            wide[pl.ds(pl.multiple_of(q * block, block), block), lev * LANES : (lev + 1) * LANES] = recv[
-                tab[source_row * devices + lev * sections + q]
-            ]
-        return carry
-
-    lax.fori_loop(0, sections, gather, 0)
-    total = split_dot(wide[...], embed_ref[...])
-    wide[:, 0:padded] = total
-
-    def divide(q, carry):
-        denom = jnp.zeros((1, padded), jnp.float32)
-        for lev in range(NLEV):
-            denom = denom + cover_ref[lev : lev + 1, :] * tab[
-                3 * devices + lev * sections + q
-            ].astype(jnp.float32)
-        inverse = 1.0 / jnp.where(denom > 0.0, denom, 1.0)
-        at = pl.multiple_of(q * block, block)
-        value = wide[pl.ds(at, block), 0:padded] * inverse
-        wide[pl.ds(at, block), 0:padded] = value
-        if keep:
-            keep_ref[q] = value
-        return carry
-
-    lax.fori_loop(0, sections, divide, 0)
-    picked = split_dot(wide[:, 0:padded], take_ref[...])
-    for lev in range(NLEV):
-        packs[pl.ds(lev * sections, sections)] = picked[:, lev * LANES : (lev + 1) * LANES].reshape(
-            sections, block, LANES
-        )
-
-    def start_second(k, carry):
-        i = far_first(k)
-        to = lax.rem(me + i, devices)
-        send2[to] = packs[tab[2 * devices + to]]
-        copy_of(send2, out_ref, 2, i).start()
-        return carry
-
-    lax.fori_loop(0, devices - 1, start_second, 0)
-    out_ref[me] = packs[tab[2 * devices + me]]
-
-    def wait_second(i, carry):
-        copy_of(send2, out_ref, 2, i).wait()
-        return carry
-
-    lax.fori_loop(1, devices, wait_second, 0)
+            packs[pl.ds(lev * sections, sections)] = picked[
+                :, lev * LANES : (lev + 1) * LANES
+            ].reshape(sections, part_cols, LANES)
+
+        def answer(across, j):
+            to = partner(across, j)
+            send2[to, cols] = packs[tab[2 * devices + to]]
+            copy_of(send2, out_ref, 1, part, across, j).start()
+
+        each_partner(answer)
+        out_ref[me, cols] = packs[tab[2 * devices + me]]
+
+    if keep:
+        for q in range(sections):
+            keep_ref[:, q * section_rows : (q + 1) * section_rows] = kept[q, :, 0:section_rows]
+    for part in range(parts):
+        each_partner(lambda across, j: copy_of(send2, out_ref, 1, part, across, j).wait())
 
 
 def local(start_field, col_speed, row_speed, levels, coeffs, assign_first, assign_second, owner_of):
@@ -394,6 +403,7 @@
     cells, lanes = start_field.shape[1:]
     block = cells // devices
     sections = devices // NLEV
+    parts = 2 if block % 16 == 0 else 1
     columns = jnp.broadcast_to(col_speed[:, None], (cells, lanes))
 
     def stage(x, assign, assign_next, count, pre, post, in_map, out_map, tables):
@@ -425,18 +435,21 @@
     def exchange(x, tab, source_row, keep, collective_id):
         outs = [jax.ShapeDtypeStruct((devices, block, lanes), jnp.float32)]
         if keep:
-            outs.append(jax.ShapeDtypeStruct((sections, block, padded), jnp.float32))
+            outs.append(jax.ShapeDtypeStruct((block, sections * section_rows), jnp.float32))
         return pl.pallas_call(
-            functools.partial(exchange_kernel, source_row, keep, devices),
+            functools.partial(exchange_kernel, source_row, keep, devices, parts, section_rows),
             out_shape=outs,
             in_specs=[SMEM_SPEC] + [VMEM_SPEC] * 4,
             out_specs=[VMEM_SPEC] * len(outs),
             scratch_shapes=[
+            ]
+            + [pltpu.VMEM((devices, block // parts, lanes), jnp.float32)] * parts
+            + [
+                pltpu.VMEM((sections * block // parts, NLEV * lanes), jnp.float32),
+                pltpu.VMEM((devices, block // parts, lanes), jnp.float32),
                 pltpu.VMEM((devices, block, lanes), jnp.float32),
-                pltpu.VMEM((sections * block, NLEV * lanes), jnp.float32),
-                pltpu.VMEM((devices, block, lanes), jnp.float32),
-                pltpu.VMEM((devices, block, lanes), jnp.float32),
-                pltpu.SemaphoreType.DMA((4, devices)),
+                pltpu.VMEM((sections, block, padded), jnp.float32),
+                pltpu.SemaphoreType.DMA((4 * parts, devices)),
             ],
             compiler_params=pltpu.CompilerParams(
                 collective_id=collective_id, has_side_effects=True
@@ -450,11 +463,8 @@
     (outgoing,) = stage(
         restricted, assign_second, assign_second, STEPS, True, True, False, True, False
     )
-    restricted, kept = exchange(outgoing, tab, 1, True, 1)
+    restricted, combined = exchange(outgoing, tab, 1, True, 1)
     (final,) = stage(restricted, assign_second, assign_second, 1, True, False, True, False, False)
-    combined = jnp.transpose(kept[:, :, :section_rows], (1, 0, 2)).reshape(
-        block, sections * section_rows
-    )
     return combined, final
 
 

time: 112 us -> 109 us (0.973); the launches traced: 114 us -> 107 us
  Pallas kernels: 110 us -> 104 us
  local copies, waits for them, and re-layouts: 3.95 us -> 2.41 us
    pallas_call x3, Pallas kernels: 43.2 us -> 23.1 us  [stage(): pl.pallas_call(functools.partial(local_kernel, count, pre, post, in_map,...]
    pallas_call x2, Pallas kernels: 66.5 us -> 81.1 us  [exchange(): pl.pallas_call(functools.partial(exchange_kernel, source_row, keep, devic...]
    transpose x2 -> x0, local copies, waits for them, and re-layouts: 1.28 us -> none  [local(): jnp.transpose(kept[:, :, :section_rows], (1, 0, 2))]
where the time goes in v3:
time: 109 us; the launch traced here: 107 us
  Pallas kernels  104 us (95%)
  local copies, waits for them, and re-layouts  2.41 us (2%)
    pallas_call x2, Pallas kernels, exchange(): pl.pallas_call(functools.partial(exchange_kernel, source_row, keep, devic...  81.1 us
    pallas_call x3, Pallas kernels, stage(): pl.pallas_call(functools.partial(local_kernel, count, pre, post, in_map,...  23.1 us

profile of v3, /device:TPU:1, one launch (start us, length us, event | category | flops | bytes accessed | tf_op | source)
XLA Modules:
  0.0 107.3 jit_solution(14211211813692520825)
XLA Ops:
  0.6 1.7 %broadcast_in_dim.2.col_ref = f32[1024,128]{1,0:T(8,128)} broadcast(f32[1024]{0:T(1024)} %param.15), dimensions={0} | broadcast | bytes 528384 | tf_op jit(solution)/shard_map/broadcast_in_dim | solution.py:407
  2.3 5.4 %shard_map.149 = (f32[16,64,128]{2,1,0:T(8,128)}, s32[64]{0:T(128)}) custom-call(s32[16]{0:T(128)} %levels.5, s32[16]{0:T(128)} %coeffs.5, s32[16]{0:T(128)} %assign.3, s32[16]{0:T(128)} %assign_next.5, s32[16]{0:T(128)} %owner.5, f32[32]{0:T(128)} %row_speed.5, f32[1,1024,128]{2,1,0:T(8,128)} %x_ref.1, f32[1024,128]{1,0:T(8,128)} %broadcast_in_dim.2.col_ref, ...), custom_call_target="tpu_custom_call" | custom-call | tf_op jit(solution)/shard_map/pallas_call | solution.py:424
  7.7 43.7 %shard_map.150.x_ref = f32[16,64,128]{2,1,0:T(8,128)} custom-call(s32[64]{0:T(128)} %get-tuple-element.6.tab, f32[16,64,128]{2,1,0:T(8,128)} %get-tuple-element.7.x_ref, bf16[512,384]{1,0:T(8,128)(2,1)} %constant.14.clone.embed_ref, bf16[384,512]{1,0:T(8,128)(2,1)} %constant.15.clone.take_ref, f32[4,384]{1,0:T(4,128)} %constant.16.clone.cover_ref), custom_call_target="tpu_custom_call" | custom-call | tf_op jit(solution)/shard_map/pallas_call | solution.py:439
  51.4 10.9 %shard_map.151.x_ref = f32[16,64,128]{2,1,0:T(8,128)} custom-call(s32[16]{0:T(128)} %levels.5, s32[16]{0:T(128)} %coeffs.5, s32[16]{0:T(128)} %assign_next.5, s32[16]{0:T(128)} %assign_next.5, s32[16]{0:T(128)} %owner.5, f32[32]{0:T(128)} %row_speed.5, f32[16,64,128]{2,1,0:T(8,128)} %shard_map.150.x_ref, f32[1024,128]{1,0:T(8,128)} %broadcast_in_dim.2.col_ref, ...), custom_call_target="tpu_custom_call" | custom-call | tf_op jit(solution)/shard_map/pallas_call | solution.py:424
  62.2 37.4 %shard_map.152 = (f32[16,64,128]{2,1,0:T(8,128)}, f32[64,1280]{1,0:T(8,128)}) custom-call(s32[64]{0:T(128)} %get-tuple-element.6.tab, f32[16,64,128]{2,1,0:T(8,128)} %shard_map.151.x_ref, bf16[512,384]{1,0:T(8,128)(2,1)} %constant.14.clone.embed_ref, bf16[384,512]{1,0:T(8,128)(2,1)} %constant.15.clone.take_ref, f32[4,384]{1,0:T(4,128)} %constant.16.clone.cover_ref), custom_call_target="tpu_custom_call" | custom-call | tf_op jit(solution)/shard_map/pallas_call | solution.py:439
  99.7 0.0 copy-start
  99.7 6.8 %shard_map.153 = f32[1,1024,128]{2,1,0:T(8,128)} custom-call(s32[16]{0:T(128)} %levels.5, s32[16]{0:T(128)} %coeffs.5, s32[16]{0:T(128)} %assign_next.5, s32[16]{0:T(128)} %assign_next.5, s32[16]{0:T(128)} %owner.5, f32[32]{0:T(128)} %row_speed.5, f32[16,64,128]{2,1,0:T(8,128)} %get-tuple-element.9.x_ref, f32[1024,128]{1,0:T(8,128)} %broadcast_in_dim.2.col_ref, ...), custom_call_target="tpu_custom_call" | custom-call | tf_op jit(solution)/shard_map/pallas_call | solution.py:424
  106.5 0.0 copy-done
  106.5 0.7 copy.17
Async XLA Ops:
  99.7 6.8 %copy-start = (f32[64,1280]{1,0:T(8,128)S(1)}, f32[64,1280]{1,0:T(8,128)}, u32[]{:S(2)}) copy-start(f32[64,1280]{1,0:T(8,128)} %get-tuple-element.12) | copy-start | bytes 983044

commit v4 on v3

--- a/solution.py
+++ b/solution.py
@@ -207,11 +207,14 @@
         row_factor = jnp.where(sample_at == f, row_speed[f], row_factor)
     row_factor = row_factor * (dt * 0.5 * scale_one)
 
-    def speeds(i, carry):
-        at = pl.multiple_of(i * 32, 32)
-        speed[pl.ds(at, 32), :] = col_ref[pl.ds(at, 32), :] * jnp.concatenate([row_factor] * 4, axis=0)
-        return carry
-    lax.fori_loop(0, cells // 32, speeds, 0)
+    for at in range(0, cells, 256):
+        speed[pl.ds(at, 256), :] = lax.dot_general(
+            col_ref[:, at : at + 256],
+            row_factor[0:1, :],
+            (((0,), (0,)), ((), ())),
+            precision=lax.Precision.HIGHEST,
+            preferred_element_type=jnp.float32,
+        )
 
     if pre:
         def take(b, carry):
@@ -228,7 +231,7 @@
         buf[pl.ds(0, cells), :] = x_ref[0]
         start = 0
 
-    group = 8
+    group = 16
     rows = group * SIDE
 
     def substep(turn, parity):
@@ -404,7 +407,7 @@
     block = cells // devices
     sections = devices // NLEV
     parts = 2 if block % 16 == 0 else 1
-    columns = jnp.broadcast_to(col_speed[:, None], (cells, lanes))
+    columns = col_speed.reshape(1, cells)
 
     def stage(x, assign, assign_next, count, pre, post, in_map, out_map, tables):
         args = [levels, coeffs, assign, assign_next, owner_of, row_speed, x, columns, stencils]

time: 109 us -> 96.5 us (0.89)
  Pallas kernels: 104 us -> 94.4 us
  local copies, waits for them, and re-layouts: 2.41 us -> 0.73 us
    pallas_call x2, Pallas kernels: 81.1 us -> 71.5 us  [exchange(): pl.pallas_call(functools.partial(exchange_kernel, source_row, keep, devic...]
    broadcast_in_dim x1 -> x0, local copies, waits for them, and re-layouts: 1.68 us -> none  [local(): columns = jnp.broadcast_to(col_speed[:, None], (cells, lanes))]
where the time goes in v4:
time: 96.5 us; the launch traced here: 95.8 us
  Pallas kernels  94.4 us (98%)
    pallas_call x2, Pallas kernels, exchange(): pl.pallas_call(functools.partial(exchange_kernel, source_row, keep, devic...  71.5 us
    pallas_call x3, Pallas kernels, stage(): pl.pallas_call(functools.partial(local_kernel, count, pre, post, in_map,...  22.9 us

profile of v4, /device:TPU:1, one launch (start us, length us, event | category | flops | bytes accessed | tf_op | source)
XLA Modules:
  0.0 95.8 jit_solution(8479790130371521318)
XLA Ops:
  0.6 8.0 %shard_map.149 = (f32[16,64,128]{2,1,0:T(8,128)}, s32[64]{0:T(128)}) custom-call(s32[16]{0:T(128)} %levels.5, s32[16]{0:T(128)} %coeffs.5, s32[16]{0:T(128)} %assign.3, s32[16]{0:T(128)} %assign_next.5, s32[16]{0:T(128)} %owner.5, f32[32]{0:T(128)} %row_speed.5, f32[1,1024,128]{2,1,0:T(8,128)} %x_ref.1, f32[1,1024]{1,0:T(1,128)} %bitcast.1, ...), custom_call_target="tpu_custom_call" | custom-call | tf_op jit(solution)/shard_map/pallas_call | solution.py:427
  8.7 36.6 %shard_map.150.x_ref = f32[16,64,128]{2,1,0:T(8,128)} custom-call(s32[64]{0:T(128)} %get-tuple-element.6.tab, f32[16,64,128]{2,1,0:T(8,128)} %get-tuple-element.7.x_ref, bf16[512,384]{1,0:T(8,128)(2,1)} %constant.14.clone.embed_ref, bf16[384,512]{1,0:T(8,128)(2,1)} %constant.15.clone.take_ref, f32[4,384]{1,0:T(4,128)} %constant.16.clone.cover_ref), custom_call_target="tpu_custom_call" | custom-call | tf_op jit(solution)/shard_map/pallas_call | solution.py:442
  45.3 8.9 %shard_map.151.x_ref = f32[16,64,128]{2,1,0:T(8,128)} custom-call(s32[16]{0:T(128)} %levels.5, s32[16]{0:T(128)} %coeffs.5, s32[16]{0:T(128)} %assign_next.5, s32[16]{0:T(128)} %assign_next.5, s32[16]{0:T(128)} %owner.5, f32[32]{0:T(128)} %row_speed.5, f32[16,64,128]{2,1,0:T(8,128)} %shard_map.150.x_ref, f32[1,1024]{1,0:T(1,128)} %bitcast.2, ...), custom_call_target="tpu_custom_call" | custom-call | tf_op jit(solution)/shard_map/pallas_call | solution.py:427
  54.2 34.9 %shard_map.152 = (f32[16,64,128]{2,1,0:T(8,128)}, f32[64,1280]{1,0:T(8,128)}) custom-call(s32[64]{0:T(128)} %get-tuple-element.6.tab, f32[16,64,128]{2,1,0:T(8,128)} %shard_map.151.x_ref, bf16[512,384]{1,0:T(8,128)(2,1)} %constant.14.clone.embed_ref, bf16[384,512]{1,0:T(8,128)(2,1)} %constant.15.clone.take_ref, f32[4,384]{1,0:T(4,128)} %constant.16.clone.cover_ref), custom_call_target="tpu_custom_call" | custom-call | tf_op jit(solution)/shard_map/pallas_call | solution.py:442
  89.1 0.0 copy-start
  89.1 6.0 %shard_map.153 = f32[1,1024,128]{2,1,0:T(8,128)} custom-call(s32[16]{0:T(128)} %levels.5, s32[16]{0:T(128)} %coeffs.5, s32[16]{0:T(128)} %assign_next.5, s32[16]{0:T(128)} %assign_next.5, s32[16]{0:T(128)} %owner.5, f32[32]{0:T(128)} %row_speed.5, f32[16,64,128]{2,1,0:T(8,128)} %get-tuple-element.9.x_ref, f32[1,1024]{1,0:T(1,128)} %bitcast.3, ...), custom_call_target="tpu_custom_call" | custom-call | tf_op jit(solution)/shard_map/pallas_call | solution.py:427
  95.1 0.0 copy-done
  95.1 0.7 copy.17
Async XLA Ops:
  89.1 6.0 %copy-start = (f32[64,1280]{1,0:T(8,128)S(1)}, f32[64,1280]{1,0:T(8,128)}, u32[]{:S(2)}) copy-start(f32[64,1280]{1,0:T(8,128)} %get-tuple-element.12) | copy-start | bytes 983044
